TPU v7x, 512 devices: a whole 4x4x16 slice. The times are simulated.
512 devices in a mesh: section: 32 (over z, core), seq: 16 (over x, y).
Axes of the slice: x: 4, y: 4, z: 16, core: 2. Of those that a mesh axis runs over, the one named last changes fastest.
Arguments:
- layer_input: bfloat16 [32, 3, 4096, 768], P('section', None, 'seq'), may hold values from -6 to 6
- grad_out: bfloat16 [32, 3, 4096, 768], P('section', None, 'seq'), may hold values from -6 to 6
- gate_weight: bfloat16 [768, 768], P('seq'), may hold values from -0.21875 to 0.21875
- mix_in_right: bfloat16 [64, 64, 64], P('seq'), may hold values from -0.75 to 0.75
- mix_in_left: bfloat16 [64, 64, 64], P('seq'), may hold values from -0.75 to 0.75
- mix_out_left: bfloat16 [64, 64, 64], P('seq'), may hold values from -0.75 to 0.75
- mix_out_right: bfloat16 [64, 64, 64], P('seq'), may hold values from -0.75 to 0.75
- kernel: bfloat16 [4096, 768], P('seq'), may hold values from -5 to 5
Outputs:
- input_grad: bfloat16 [32, 3, 4096, 768], P('section', None, 'seq')
- weight_grad: float32 [768, 768], P('seq')
- kernel_grad: bfloat16 [4096, 768], P('seq')
All inputs are finite; a program needn't handle non-finite values.
Results may differ from a plain program's by a relative error of at most 0.007.
Values may be sent and summed in bfloat16 or wider, within the bound.
A program may use at most 64 MiB of HBM per device.

v0:
```python
import math
import jax
import jax.numpy as jnp
from jax import lax
from jax.sharding import PartitionSpec as P

BATCH = 3
SEQ = 4096


def contract(form, left, right):
    return jnp.einsum(form, left, right, preferred_element_type=jnp.float32)


def forward_middle(spread, left_in, left_out, kern):
    second_mixed = contract("ija,baid->bijd", left_in, spread)
    weighted = (second_mixed * kern).astype(jnp.bfloat16)
    third_mixed = contract("ikj,bijd->bikd", left_out, weighted).astype(jnp.bfloat16)
    return (second_mixed, third_mixed)


def backward_middle(back_spread, second_mixed, left_in, left_out, kern):
    back_second = contract("ikj,bkid->bijd", left_out, back_spread)
    kernel_sum = jnp.sum(second_mixed * back_second, axis=0)
    back_weighted = (back_second * kern).astype(jnp.bfloat16)
    back_first = contract("ija,bijd->biad", left_in, back_weighted).astype(jnp.bfloat16)
    return (kernel_sum, back_first)


def local(
    layer_input,
    grad_out,
    gate_weight,
    mix_in_right,
    mix_in_left,
    mix_out_left,
    mix_out_right,
    kernel,
):
    count_batch = layer_input.shape[1]
    token_rows = layer_input.shape[2]
    width = layer_input.shape[3]
    groups = mix_in_right.shape[0]
    block_size = mix_in_right.shape[1]
    replicas = lax.axis_size("section")
    kern = kernel.reshape(groups, block_size, width).astype(jnp.float32)
    acts = layer_input[0].reshape(count_batch, groups, block_size, width)
    flat_input = layer_input[0].reshape(count_batch * token_rows, width)
    upstream = grad_out[0].reshape(count_batch * token_rows, width).astype(jnp.float32)
    weights = lax.all_gather(gate_weight, "seq", axis=0, tiled=True)
    preact = jnp.dot(flat_input, weights, preferred_element_type=jnp.float32)
    sigma = jax.nn.sigmoid(preact)
    swish = preact * sigma
    slope = sigma * (1.0 + preact * (1.0 - sigma))
    mix_grad = (
        (upstream * swish).astype(jnp.bfloat16).reshape(count_batch, groups, block_size, width)
    )
    first_mixed = contract("aic,bacd->baid", mix_in_right, acts).astype(jnp.bfloat16)
    back_third = contract("kmi,bkmd->bkid", mix_out_right, mix_grad).astype(jnp.bfloat16)
    spread = lax.all_to_all(first_mixed, "seq", split_axis=2, concat_axis=1, tiled=True)
    second_mixed, third_mixed = forward_middle(spread, mix_in_left, mix_out_left, kern)
    returned = lax.all_to_all(third_mixed, "seq", split_axis=2, concat_axis=1, tiled=True)
    back_spread = lax.all_to_all(back_third, "seq", split_axis=2, concat_axis=1, tiled=True)
    kernel_sum, back_first = backward_middle(
        back_spread, second_mixed, mix_in_left, mix_out_left, kern
    )
    back_return = lax.all_to_all(back_first, "seq", split_axis=2, concat_axis=1, tiled=True)
    mixed = contract("kmi,bikd->bkmd", mix_out_right, returned).reshape(
        count_batch * token_rows, width
    )
    gate_grad = (upstream * mixed * slope).astype(jnp.bfloat16)
    gate_part = lax.dot_general(
        gate_grad, weights, (((1,), (1,)), ((), ())), preferred_element_type=jnp.float32
    )
    weight_scale = 1.0 / math.sqrt(replicas * BATCH * SEQ)
    kernel_scale = 1.0 / math.sqrt(replicas * BATCH)
    term = lax.dot_general(
        flat_input, gate_grad, (((0,), (0,)), ((), ())), preferred_element_type=jnp.float32
    )
    weight_local = lax.psum_scatter(term * weight_scale, "seq", scatter_dimension=0, tiled=True)
    weight_grad, kernel_total = lax.psum((weight_local, kernel_sum * kernel_scale), "section")
    mix_part = contract("aic,biad->bacd", mix_in_right, back_return).reshape(
        count_batch * token_rows, width
    )
    input_grad = (
        (gate_part + mix_part).astype(jnp.bfloat16).reshape(1, count_batch, token_rows, width)
    )
    kernel_grad = kernel_total.astype(jnp.bfloat16).reshape(groups * block_size, width)
    return (input_grad, weight_grad, kernel_grad)


def solution(mesh):
    placed = (
        P("section", None, "seq", None),
        P("section", None, "seq", None),
        P("seq", None),
        P("seq", None, None),
        P("seq", None, None),
        P("seq", None, None),
        P("seq", None, None),
        P("seq", None),
    )
    return jax.shard_map(
        local,
        mesh=mesh,
        in_specs=placed,
        out_specs=(P("section", None, "seq", None), P("seq", None), P("seq", None)),
        check_vma=False,
    )
```

profile of v0, /device:TPU:2, one launch (start us, length us, event | category | flops | bytes accessed | tf_op | source)
XLA Modules:
  0.0 457.6 jit_solution(12352171297710613128)
XLA Ops:
  9.7 1.9 copy.54
  11.7 9.5 %all-to-all-start = ((bf16[3,4,64,768]{3,1,0,2:T(4,128)(2,1)}), bf16[3,4,64,768]{3,1,0,2:T(4,128)(2,1)S(1)}, u32[]{:S(2)}, u32[]{:S(2)}) async-start(bf16[3,4,64,768]{3,1,0,2:T(4,128)(2,1)} %copy.54), calls=%async_computation | async-start | bytes 2359296 | tf_op jit(solution)/shard_map/all_to_all | solution.py:60
  22.9 13.2 %all-to-all-done = bf16[3,4,64,768]{3,1,0,2:T(4,128)(2,1)S(1)} async-done(((bf16[3,4,64,768]{3,1,0,2:T(4,128)(2,1)}), bf16[3,4,64,768]{3,1,0,2:T(4,128)(2,1)S(1)}, u32[]{:S(2)}, u32[]{:S(2)}) %all-to-all-start) | async-done | bytes 1179680 | tf_op jit(solution)/shard_map/all_to_all | solution.py:60
  37.8 1.8 fusion.23
  41.1 22.2 %all_to_all.72 = bf16[3,4,64,768]{3,1,0,2:T(4,128)(2,1)S(1)} all-to-all(bf16[3,4,64,768]{3,1,0,2:T(4,128)(2,1)S(1)} %copy.56), channel_id=1, replica_groups=mesh['section'=32,'seq'=16] {'seq'}, dimensions={2} | all-to-all | bytes 2359296 | tf_op jit(solution)/shard_map/all_to_all | solution.py:62
  63.2 1.5 copy.98
  64.8 3.1 all_to_all.59
  67.9 1.8 convolution_bitcast_fusion
  69.7 1.6 copy.58
  71.2 18.5 %all-gather.2.cloned.1.call-done = bf16[768,768]{1,0:T(8,128)(2,1)} async-done(((bf16[48,768]{1,0:T(8,128)(2,1)}), bf16[768,768]{1,0:T(8,128)(2,1)}) %all-gather.2.cloned.1.call-update) | async-done | bytes 1179664 | tf_op jit(solution)/shard_map/all_gather | solution.py:50
  89.7 5.1 %fusion.1 = (bf16[768,768]{1,0:T(8,128)(2,1)S(1)}, bf16[768,768]{1,0:T(8,128)(2,1)}) fusion(f32[3,4,64,768]{3,2,1,0:T(8,128)} %copy.58, bf16[1,3,256,768]{3,2,1,0:T(8,128)(2,1)} %param.9, bf16[768,768]{1,0:T(8,128)(2,1)S(1)} %bitcast.123, bf16[768,768]{1,0:T(8,128)(2,1)} %all-gather.2.cloned.1.call-done), kind=kOutput, calls=%fused_computation.3 | convolution fusion | flops 914227200 | bytes 8257536 | tf_op jit(solution)/shard_map/dot_general | solution.py:51
  95.9 2.5 multiply_bitcast_fusion
  98.4 3.1 copy.86
  101.5 1.8 fusion.7
  104.2 22.5 %all_to_all.73 = bf16[3,4,64,768]{3,1,0,2:T(4,128)(2,1)S(1)} all-to-all(bf16[3,4,64,768]{3,1,0,2:T(4,128)(2,1)S(1)} %copy.61), channel_id=1, replica_groups=mesh['section'=32,'seq'=16] {'seq'}, dimensions={2} | all-to-all | bytes 2359296 | tf_op jit(solution)/shard_map/all_to_all | solution.py:63
  128.3 3.2 all_to_all.63
  131.5 2.8 fusion.5
  134.8 1.9 copy.65
  136.8 5.5 %all-to-all-start.3 = ((bf16[3,4,64,768]{3,1,0,2:T(4,128)(2,1)}), bf16[3,4,64,768]{3,1,0,2:T(4,128)(2,1)S(1)}, u32[]{:S(2)}, u32[]{:S(2)}) async-start(bf16[3,4,64,768]{3,1,0,2:T(4,128)(2,1)} %copy.65), calls=%async_computation.3 | async-start | bytes 2359296 | tf_op jit(solution)/shard_map/all_to_all | solution.py:67
  143.2 100.1 %all-reduce.4 = bf16[4,64,768]{2,1,0:T(8,128)(2,1)} all-reduce(f32[4,64,768]{2,1,0:T(8,128)} %broadcast_multiply_fusion), channel_id=1, replica_groups=mesh['section'=32,'seq'=16] {'section'}, use_global_device_ids=true, to_apply=%region_3.0 | all-reduce | flops 196608 | bytes 1179648 | tf_op jit(solution)/shard_map/psum | solution.py:81
  245.7 1.8 copy.87
  247.6 3.8 fusion.3
  251.3 198.0 %all-reduce.3.cloned.1.call-done = f32[48,768]{0,1:T(8,128)} async-done(((f32[48,768]{0,1:T(8,128)}), f32[48,768]{0,1:T(8,128)}) %all-reduce.3.cloned.1.call-update) | async-done | bytes 147472 | tf_op jit(solution)/shard_map/psum | solution.py:81
  449.3 1.8 copy.69
  (38 shorter events, 14.7 us)
Async XLA Ops:
  7.2 1.3 copy-start
  11.7 10.3 %copy-start.4 = (bf16[256,768]{1,0:T(8,128)(2,1)S(1)}, bf16[256,768]{1,0:T(8,128)(2,1)}, u32[]{:S(2)}) copy-start(bf16[256,768]{1,0:T(8,128)(2,1)} %param.15) | copy-start | bytes 1179652
  11.7 24.5 %all-to-all-start = ((bf16[3,4,64,768]{3,1,0,2:T(4,128)(2,1)}), bf16[3,4,64,768]{3,1,0,2:T(4,128)(2,1)S(1)}, u32[]{:S(2)}, u32[]{:S(2)}) async-start(bf16[3,4,64,768]{3,1,0,2:T(4,128)(2,1)} %copy.54), calls=%async_computation | async-start | bytes 2359296 | tf_op jit(solution)/shard_map/all_to_all | solution.py:60
  21.2 68.5 %all-gather.2.cloned.1.call-start = ((), (), s32[]{:S(2)}) async-start(), calls=%async_computation.5 | async-start | bytes 1253376 | tf_op jit(solution)/shard_map/all_gather | solution.py:50
  21.9 223.8 %reduce-scatter.4.cloned.1.call-start = ((), (), s32[]{:S(2)}) async-start(), calls=%async_computation.7 | async-start | bytes 2506752
  37.8 1.8 copy-start.1
  37.8 1.8 copy-start.5
  94.9 1.1 copy-start.7
  131.5 2.8 copy-start.2
  131.5 2.8 copy-start.6
  136.8 5.5 %copy-start.3 = (f32[4,64,768]{2,1,0:T(8,128)S(1)}, f32[4,64,768]{2,1,0:T(8,128)}, u32[]{:S(2)}) copy-start(f32[4,64,768]{2,1,0:T(8,128)} %get-tuple-element.17) | copy-start | bytes 2359300
  136.8 106.6 %all-to-all-start.3 = ((bf16[3,4,64,768]{3,1,0,2:T(4,128)(2,1)}), bf16[3,4,64,768]{3,1,0,2:T(4,128)(2,1)S(1)}, u32[]{:S(2)}, u32[]{:S(2)}) async-start(bf16[3,4,64,768]{3,1,0,2:T(4,128)(2,1)} %copy.65), calls=%async_computation.3 | async-start | bytes 2359296 | tf_op jit(solution)/shard_map/all_to_all | solution.py:67
  142.2 307.1 %all-reduce.3.cloned.1.call-start = ((), (), s32[]{:S(2)}) async-start(), calls=%async_computation.6 | async-start | bytes 786432 | tf_op jit(solution)/shard_map/psum | solution.py:81
Sparse Core Ops, SparseCore 0:
  25.1 64.5 all-gather.1
  101.6 98.0 reduce-scatter.3
  247.7 201.5 all-reduce.2
where the time goes:
time: 459 us; the launch traced here: 458 us
  waiting for transfers between devices  230 us (50%)
  blocking collectives  145 us (32%)
  local copies, waits for them, and re-layouts  28.3 us (6%)
  matrix products  23.3 us (5%)
  starting transfers between devices  15.1 us (3%)
  between operations  13.9 us (3%)
    psum x1, waiting for transfers between devices, local(): lax.psum((weight_local, kernel_sum * kernel_scale), 'section')  198 us
    psum x1, blocking collectives, local(): lax.psum((weight_local, kernel_sum * kernel_scale), 'section')  100 us
    all_to_all x1, blocking collectives, local(): lax.all_to_all(back_third, 'seq', split_axis=2, concat_axis=1, tiled=True)  22.5 us
    all_to_all x1, blocking collectives, local(): lax.all_to_all(third_mixed, 'seq', split_axis=2, concat_axis=1, tiled=True)  22.2 us
    all_gather x1, waiting for transfers between devices, local(): weights = lax.all_gather(gate_weight, 'seq', axis=0, tiled=True)  18.5 us
    all_to_all x1, waiting for transfers between devices, local(): lax.all_to_all(first_mixed, 'seq', split_axis=2, concat_axis=1, tiled=True)  13.2 us
    dot_general x8, matrix products, contract(): return jnp.einsum(form, left, right, preferred_element_type=jnp.float32)  11.8 us
    all_to_all x1, starting transfers between devices, local(): lax.all_to_all(first_mixed, 'seq', split_axis=2, concat_axis=1, tiled=True)  9.55 us
  transfers between devices with their start and end apart: 5, of which 3 were waited for; matrix products, arithmetic and copies ran while one was open for 6% of the time, Pallas kernels for 0%

commit v1 on v0

--- a/solution.py
+++ b/solution.py
@@ -59,7 +59,12 @@
     back_third = contract("kmi,bkmd->bkid", mix_out_right, mix_grad).astype(jnp.bfloat16)
     spread = lax.all_to_all(first_mixed, "seq", split_axis=2, concat_axis=1, tiled=True)
     second_mixed, third_mixed = forward_middle(spread, mix_in_left, mix_out_left, kern)
-    returned = lax.all_to_all(third_mixed, "seq", split_axis=2, concat_axis=1, tiled=True)
+    returned = jnp.concatenate(
+        lax.all_to_all(
+            jnp.stack(jnp.split(third_mixed, lax.axis_size("seq"), axis=2)), "seq", 0, 0
+        ),
+        axis=1,
+    )
     back_spread = lax.all_to_all(back_third, "seq", split_axis=2, concat_axis=1, tiled=True)
     kernel_sum, back_first = backward_middle(
         back_spread, second_mixed, mix_in_left, mix_out_left, kern

time: 459 us -> 459 us (level)
  waiting for transfers between devices: 230 us -> 236 us
  local copies, waits for them, and re-layouts: 28.3 us -> 23.4 us
    all_gather x1, waiting for transfers between devices: 18.5 us -> 24.6 us  [local(): weights = lax.all_gather(gate_weight, 'seq', axis=0, tiled=True)]
    all_to_all x2 -> x0, local copies, waits for them, and re-layouts: 4.69 us -> none  [local(): lax.all_to_all(third_mixed, 'seq', split_axis=2, concat_axis=1, tiled=True)]
    unnamed x19 -> x36, local copies, waits for them, and re-layouts: 9.03 us -> 9.72 us
  transfers between devices with their start and end apart: 5 -> 5, of which waited for: 3 -> 3; matrix products, arithmetic and copies ran while one was open for 6% -> 5% of each run, Pallas kernels for 0% -> 0%
where the time goes in v1:
time: 459 us; the launch traced here: 458 us
  waiting for transfers between devices  236 us (51%)
  blocking collectives  146 us (32%)
  local copies, waits for them, and re-layouts  23.4 us (5%)
  matrix products  22 us (5%)
  starting transfers between devices  15.1 us (3%)
  between operations  13.9 us (3%)
    psum x1, waiting for transfers between devices, local(): lax.psum((weight_local, kernel_sum * kernel_scale), 'section')  197 us
    psum x1, blocking collectives, local(): lax.psum((weight_local, kernel_sum * kernel_scale), 'section')  101 us
    all_gather x1, waiting for transfers between devices, local(): weights = lax.all_gather(gate_weight, 'seq', axis=0, tiled=True)  24.6 us
    all_to_all x1, blocking collectives, local(): lax.all_to_all(back_third, 'seq', split_axis=2, concat_axis=1, tiled=True)  22.5 us
    all_to_all x1, blocking collectives, local(): lax.all_to_all(jnp.stack(jnp.split(third_mixed, lax.axis_size('seq'), axi...  22.3 us
    all_to_all x1, waiting for transfers between devices, local(): lax.all_to_all(first_mixed, 'seq', split_axis=2, concat_axis=1, tiled=True)  13.2 us
    dot_general x8, matrix products, contract(): return jnp.einsum(form, left, right, preferred_element_type=jnp.float32)  10.5 us
    unnamed x36, local copies, waits for them, and re-layouts  9.72 us
  transfers between devices with their start and end apart: 5, of which 3 were waited for; matrix products, arithmetic and copies ran while one was open for 5% of the time, Pallas kernels for 0%

profile of v1, /device:TPU:2, one launch (start us, length us, event | category | flops | bytes accessed | tf_op | source)
XLA Modules:
  0.0 458.2 jit_solution(2591197787290859556)
XLA Ops:
  8.4 1.3 fusion.9
  9.7 1.9 copy.53
  11.7 9.5 %all-to-all-start = ((bf16[3,4,64,768]{3,1,0,2:T(4,128)(2,1)}), bf16[3,4,64,768]{3,1,0,2:T(4,128)(2,1)S(1)}, u32[]{:S(2)}, u32[]{:S(2)}) async-start(bf16[3,4,64,768]{3,1,0,2:T(4,128)(2,1)} %copy.53), calls=%async_computation | async-start | bytes 2359296 | tf_op jit(solution)/shard_map/all_to_all | solution.py:60
  22.9 13.2 %all-to-all-done = bf16[3,4,64,768]{3,1,0,2:T(4,128)(2,1)S(1)} async-done(((bf16[3,4,64,768]{3,1,0,2:T(4,128)(2,1)}), bf16[3,4,64,768]{3,1,0,2:T(4,128)(2,1)S(1)}, u32[]{:S(2)}, u32[]{:S(2)}) %all-to-all-start) | async-done | bytes 1179680 | tf_op jit(solution)/shard_map/all_to_all | solution.py:60
  37.8 1.8 fusion.40
  40.9 22.3 %all_to_all.59 = bf16[16,3,4,4,768]{4,3,1,2,0:T(4,128)(2,1)S(1)} all-to-all(bf16[16,3,4,4,768]{4,3,1,2,0:T(4,128)(2,1)S(1)} %fusion.18), channel_id=1, replica_groups=mesh['section'=32,'seq'=16] {'seq'}, dimensions={0} | all-to-all | bytes 2359296 | tf_op jit(solution)/shard_map/all_to_all | solution.py:63
  63.7 1.6 copy.56
  65.2 24.6 %all-gather.2.cloned.1.call-done = bf16[768,768]{1,0:T(8,128)(2,1)} async-done(((bf16[48,768]{1,0:T(8,128)(2,1)}), bf16[768,768]{1,0:T(8,128)(2,1)}) %all-gather.2.cloned.1.call-update) | async-done | bytes 1179664 | tf_op jit(solution)/shard_map/all_gather | solution.py:50
  89.8 5.1 %fusion.1 = (bf16[768,768]{1,0:T(8,128)(2,1)S(1)}, bf16[768,768]{1,0:T(8,128)(2,1)}) fusion(f32[3,4,64,768]{3,2,1,0:T(8,128)} %copy.56, bf16[1,3,256,768]{3,2,1,0:T(8,128)(2,1)} %param.9, bf16[768,768]{1,0:T(8,128)(2,1)S(1)} %bitcast.183, bf16[768,768]{1,0:T(8,128)(2,1)} %all-gather.2.cloned.1.call-done), kind=kOutput, calls=%fused_computation.3 | convolution fusion | flops 914227200 | bytes 8257536 | tf_op jit(solution)/shard_map/dot_general | solution.py:51
  96.1 2.5 multiply_bitcast_fusion
  98.6 3.1 copy.84
  101.7 1.8 fusion.7
  104.4 22.5 %all_to_all.60 = bf16[3,4,64,768]{3,1,0,2:T(4,128)(2,1)S(1)} all-to-all(bf16[3,4,64,768]{3,1,0,2:T(4,128)(2,1)S(1)} %copy.59), channel_id=1, replica_groups=mesh['section'=32,'seq'=16] {'seq'}, dimensions={2} | all-to-all | bytes 2359296 | tf_op jit(solution)/shard_map/all_to_all | solution.py:68
  126.9 1.5 copy.96
  128.4 3.2 all_to_all.50
  131.6 2.8 fusion.5
  135.0 1.9 copy.63
  136.9 5.5 %all-to-all-start.3 = ((bf16[3,4,64,768]{3,1,0,2:T(4,128)(2,1)}), bf16[3,4,64,768]{3,1,0,2:T(4,128)(2,1)S(1)}, u32[]{:S(2)}, u32[]{:S(2)}) async-start(bf16[3,4,64,768]{3,1,0,2:T(4,128)(2,1)} %copy.63), calls=%async_computation.3 | async-start | bytes 2359296 | tf_op jit(solution)/shard_map/all_to_all | solution.py:72
  143.4 101.1 %all-reduce.4 = bf16[4,64,768]{2,1,0:T(8,128)(2,1)} all-reduce(f32[4,64,768]{2,1,0:T(8,128)} %broadcast_multiply_fusion), channel_id=1, replica_groups=mesh['section'=32,'seq'=16] {'section'}, use_global_device_ids=true, to_apply=%region_3.0 | all-reduce | flops 196608 | bytes 1179648 | tf_op jit(solution)/shard_map/psum | solution.py:86
  245.4 1.4 convolution_bitcast_fusion.1
  246.9 1.8 copy.85
  248.8 3.8 fusion.3
  252.5 197.3 %all-reduce.3.cloned.1.call-done = f32[48,768]{0,1:T(8,128)} async-done(((f32[48,768]{0,1:T(8,128)}), f32[48,768]{0,1:T(8,128)}) %all-reduce.3.cloned.1.call-update) | async-done | bytes 147472 | tf_op jit(solution)/shard_map/psum | solution.py:86
  449.8 1.8 copy.67
  (53 shorter events, 10.8 us)
Async XLA Ops:
  7.2 1.3 copy-start
  11.7 10.3 %copy-start.4 = (bf16[256,768]{1,0:T(8,128)(2,1)S(1)}, bf16[256,768]{1,0:T(8,128)(2,1)}, u32[]{:S(2)}) copy-start(bf16[256,768]{1,0:T(8,128)(2,1)} %param.15) | copy-start | bytes 1179652
  11.7 24.5 %all-to-all-start = ((bf16[3,4,64,768]{3,1,0,2:T(4,128)(2,1)}), bf16[3,4,64,768]{3,1,0,2:T(4,128)(2,1)S(1)}, u32[]{:S(2)}, u32[]{:S(2)}) async-start(bf16[3,4,64,768]{3,1,0,2:T(4,128)(2,1)} %copy.53), calls=%async_computation | async-start | bytes 2359296 | tf_op jit(solution)/shard_map/all_to_all | solution.py:60
  21.2 68.6 %all-gather.2.cloned.1.call-start = ((), (), s32[]{:S(2)}) async-start(), calls=%async_computation.5 | async-start | bytes 1253376 | tf_op jit(solution)/shard_map/all_gather | solution.py:50
  21.9 225.0 %reduce-scatter.4.cloned.1.call-start = ((), (), s32[]{:S(2)}) async-start(), calls=%async_computation.7 | async-start | bytes 2506752
  37.8 1.8 copy-start.1
  37.8 1.8 copy-start.5
  40.9 22.3 %copy-start.7 = (bf16[4,64,64]{2,1,0:T(8,128)(2,1)S(1)}, bf16[4,64,64]{2,1,0:T(8,128)(2,1)}, u32[]{:S(2)}) copy-start(bf16[4,64,64]{2,1,0:T(8,128)(2,1)} %param.14) | copy-start | bytes 98308
  95.0 1.1 copy-start.8
  131.6 2.8 copy-start.2
  131.6 2.8 copy-start.6
  136.9 5.5 %copy-start.3 = (f32[4,64,768]{2,1,0:T(8,128)S(1)}, f32[4,64,768]{2,1,0:T(8,128)}, u32[]{:S(2)}) copy-start(f32[4,64,768]{2,1,0:T(8,128)} %get-tuple-element.17) | copy-start | bytes 2359300
  136.9 107.6 %all-to-all-start.3 = ((bf16[3,4,64,768]{3,1,0,2:T(4,128)(2,1)}), bf16[3,4,64,768]{3,1,0,2:T(4,128)(2,1)S(1)}, u32[]{:S(2)}, u32[]{:S(2)}) async-start(bf16[3,4,64,768]{3,1,0,2:T(4,128)(2,1)} %copy.63), calls=%async_computation.3 | async-start | bytes 2359296 | tf_op jit(solution)/shard_map/all_to_all | solution.py:72
  142.4 307.5 %all-reduce.3.cloned.1.call-start = ((), (), s32[]{:S(2)}) async-start(), calls=%async_computation.6 | async-start | bytes 786432 | tf_op jit(solution)/shard_map/psum | solution.py:86
Sparse Core Ops, SparseCore 0:
  25.1 64.6 all-gather.1
  101.8 97.1 reduce-scatter.3
  248.9 200.9 all-reduce.2
